TPU v7x, 512 devices: a whole 4x4x16 slice. The times are simulated.
512 devices in a mesh: blk: 64 (over z, x_lo, core), rep: 8 (over y, x_hi).
Axes of the slice: x: 4 (x_hi: 2, x_lo: 2; x = x_hi * 2 + x_lo), y: 4, z: 16, core: 2. Of those that a mesh axis runs over, the one named last changes fastest.
Arguments:
- features: bfloat16 [65536, 256], P(('blk', 'rep')), may hold values from -6 to 6
- out_grad: bfloat16 [65536, 256], P('blk'), may hold values from -4 to 4
- weight: bfloat16 [256, 256], replicated, may hold values from -0.375 to 0.375
- block_words: int32 [64, 64, 8, 16, 128], P('blk', 'rep'), may hold values from 0 to 255
- block_coords: int32 [64, 64, 2, 8], P('blk', 'rep'), may hold values from 0 to 7, as said below
- block_counts: int32 [64, 64], P('blk', 'rep'), may hold values from 1 to 8, as said below
- degrees: int32 [65536], P('blk'), may hold values from 1 to 127
Outputs:
- input_grad: bfloat16 [65536, 256], P(('blk', 'rep'))
- weight_grad: float32 [256, 256], replicated
Inputs may be any that keep to these rules, and one draw needn't show every extreme that they name: `block_coords`: within one slab pair the 8 slots name distinct pairs of row block and column block. `block_counts`: the 8 slab pairs of one device include one in which all 8 slots are live.
All inputs are finite; a program needn't handle non-finite values.
Results may differ from a plain program's by a relative error of at most 0.015.
Values may be sent and summed in bfloat16 or wider, within the bound.
A program may use at most 64 MiB of HBM per device.

v0:
```python
import math
import jax
import jax.numpy as jnp
from jax import lax
from jax.sharding import PartitionSpec as P


def from_behind(block, axis, distance):
    devices = range(lax.axis_size(axis))
    route = [((i - distance) % len(devices), i) for i in devices]
    return lax.ppermute(block, axis, route)


def unpack_block(slot_words):
    shifts = jnp.arange(8, dtype=jnp.int32)
    bit_values = jnp.bitwise_and(
        jnp.right_shift(slot_words[:, :, None, :], shifts[None, None, :, None]), 1
    )
    return bit_values.reshape(slot_words.shape[0], 128, 128).astype(jnp.bfloat16)


def per_device(features, out_grad, weight, block_words, block_coords, block_counts, degrees):
    slab_rows, width = out_grad.shape
    row_blocks = slab_rows // 128
    group_size = lax.axis_size("rep")
    step_count = lax.axis_size("blk") // group_size
    rep_index = lax.axis_index("rep")
    inverse_root = lax.rsqrt(degrees.astype(jnp.float32))
    scaled = (out_grad.astype(jnp.float32) * inverse_root[:, None]).astype(jnp.bfloat16)
    column_ids = jnp.arange(row_blocks, dtype=jnp.int32)
    slot_total = block_words.shape[2]
    slot_ids = jnp.arange(slot_total, dtype=jnp.int32)

    def add_slot(accumulated, source_slab, slot_index):
        slot_words = lax.dynamic_index_in_dim(block_words[0], slot_index, 0, keepdims=False)
        coords = lax.dynamic_index_in_dim(block_coords[0], slot_index, 0, keepdims=False)
        live_count = lax.dynamic_index_in_dim(block_counts[0], slot_index, 0, keepdims=False)
        picked = jnp.take(source_slab.reshape(row_blocks, 128, width), coords[0], axis=0)
        transposed = unpack_block(slot_words)
        contrib = jnp.einsum("bvu,buf->bvf", transposed, picked, preferred_element_type=jnp.float32)
        live_slots = slot_ids < live_count
        placement = ((coords[1][:, None] == column_ids[None, :]) & live_slots[:, None]).astype(
            jnp.float32
        )
        return accumulated + jnp.einsum("bc,bvf->cvf", placement, contrib)

    empty = jnp.zeros((row_blocks, 128, width), jnp.float32)
    current = scaled
    for bit in range(group_size.bit_length() - 1):
        shifted = from_behind(current, "blk", -(1 << bit) * step_count)
        current = jnp.where(
            jnp.bitwise_and(jnp.right_shift(rep_index, bit), 1) == 1, shifted, current
        )
    accumulated = add_slot(empty, current, 0)

    def advance(step_index, state_tuple):
        current, accumulated = state_tuple
        current = from_behind(current, "blk", -1)
        return (current, add_slot(accumulated, current, step_index))

    current, accumulated = lax.fori_loop(1, step_count, advance, (current, accumulated))
    partial_sums = accumulated.reshape(slab_rows, width)
    share_rows = slab_rows // group_size
    share_root = lax.dynamic_slice_in_dim(inverse_root, rep_index * share_rows, share_rows, 0)
    whole_sums = lax.psum(partial_sums, "rep")
    own_sums = lax.dynamic_slice_in_dim(whole_sums, rep_index * share_rows, share_rows, 0)
    aggregated = (own_sums * share_root[:, None]).astype(jnp.bfloat16)
    input_grad = lax.dot_general(
        aggregated, weight, (((1,), (1,)), ((), ())), preferred_element_type=jnp.float32
    ).astype(jnp.bfloat16)
    weight_term = lax.dot_general(
        features, aggregated, (((0,), (0,)), ((), ())), preferred_element_type=jnp.float32
    )
    node_total = slab_rows * lax.axis_size("blk")
    weight_grad = lax.psum(weight_term, ("blk", "rep")) * (1.0 / math.sqrt(node_total))
    return (input_grad, weight_grad)


def solution(mesh):
    return jax.shard_map(
        per_device,
        mesh=mesh,
        in_specs=(
            P(("blk", "rep"), None),
            P("blk", None),
            P(),
            P("blk", "rep", None, None, None),
            P("blk", "rep", None, None),
            P("blk", "rep"),
            P("blk"),
        ),
        out_specs=(P(("blk", "rep"), None), P()),
        check_vma=False,
    )
```

profile of v0, /device:TPU:4, one launch (start us, length us, event | category | flops | bytes accessed | tf_op | source)
XLA Modules:
  0.0 821.2 jit_solution(11861567313591803345)
XLA Ops:
  7.2 0.7 convert_rsqrt_fusion
  7.9 1.3 multiply_convert_fusion
  9.3 11.8 %collective-permute-start.1 = (bf16[1024,256]{1,0:T(8,128)(2,1)S(1)}, bf16[1024,256]{1,0:T(8,128)(2,1)S(1)}, u32[]{:S(2)}, u32[]{:S(2)}) collective-permute-start(bf16[1024,256]{1,0:T(8,128)(2,1)S(1)} %multiply_convert_fusion), channel_id=1, source_target_pairs={{64,0},{72,8},{80,16},{88,24},{96,32},{104,40},{112,48},{120,56},{... | collective-permute-start | bytes 1572872 | tf_op jit(solution)/shard_map/ppermute | solution.py:11
  21.1 22.4 %collective-permute-done.1 = bf16[1024,256]{1,0:T(8,128)(2,1)S(1)} collective-permute-done((bf16[1024,256]{1,0:T(8,128)(2,1)S(1)}, bf16[1024,256]{1,0:T(8,128)(2,1)S(1)}, u32[]{:S(2)}, u32[]{:S(2)}) %collective-permute-start.1) | collective-permute-done | bytes 524320 | tf_op jit(solution)/shard_map/ppermute | solution.py:11
  43.8 6.3 collective-permute-start.2
  50.3 0.7 compare_and_fusion.1
  51.0 40.0 %collective-permute-done.2 = bf16[1024,256]{1,0:T(8,128)(2,1)S(1)} collective-permute-done((bf16[1024,256]{1,0:T(8,128)(2,1)S(1)}, bf16[1024,256]{1,0:T(8,128)(2,1)S(1)}, u32[]{:S(2)}, u32[]{:S(2)}) %collective-permute-start.2) | collective-permute-done | bytes 524320 | tf_op jit(solution)/shard_map/ppermute | solution.py:11
  91.1 5.0 collective-permute-start.3
  96.7 0.7 slice_bitcast_fusion.2
  97.4 0.8 slice_bitcast_fusion.1
  98.3 28.4 %collective-permute-done.3 = bf16[1024,256]{1,0:T(8,128)(2,1)S(1)} collective-permute-done((bf16[1024,256]{1,0:T(8,128)(2,1)S(1)}, bf16[1024,256]{1,0:T(8,128)(2,1)S(1)}, u32[]{:S(2)}, u32[]{:S(2)}) %collective-permute-start.3) | collective-permute-done | bytes 524320 | tf_op jit(solution)/shard_map/ppermute | solution.py:11
  128.1 121.5 %while.20 = (s32[]{:T(128)}, bf16[1024,256]{1,0:T(8,128)(2,1)S(1)}, f32[8,128,256]{2,0,1:T(8,128)S(1)}, s32[1,8,2,8]{3,2,1,0:T(2,128)}, s32[1,8]{1,0:T(1,128)S(1...) while((s32[]{:T(128)}, bf16[1024,256]{1,0:T(8,128)(2,1)S(1)}, ...), condition=%wide.region_1.3_spmd.clone.clone, body=%wide.region_0.2_spmd.clone.clone.sunk | while | flops 72221880 | bytes 8067647 | solution.py:61
  128.2 29.0 %collective-permute-start = (bf16[1024,256]{1,0:T(8,128)(2,1)S(1)}, bf16[1024,256]{1,0:T(8,128)(2,1)S(1)}, u32[]{:S(2)}, u32[]{:S(2)}) collective-permute-start(bf16[1024,256]{1,0:T(8,128)(2,1)S(1)} %get-tuple-element.308), channel_id=1, source_target_pairs={{8,0},{16,8},{24,16},{32,24},{40,32},{48,40},{56,48},{64,56},{72,6... | collective-permute-start | bytes 1572872 | tf_op jit(solution)/shard_map/while/body/eval_jaxpr/ppermute | solution.py:11
  157.8 0.7 constant_dynamic-slice_fusion.4
  159.2 0.9 dynamic-slice_bitcast_fusion.2
  160.1 3.8 collective-permute-done
  165.3 5.9 collective-permute-start
  171.8 0.7 constant_dynamic-slice_fusion.4
  173.3 0.9 dynamic-slice_bitcast_fusion.2
  174.2 3.8 collective-permute-done
  179.4 5.9 collective-permute-start
  185.9 0.7 constant_dynamic-slice_fusion.4
  186.7 0.7 iota_compare_fusion.5
  187.4 0.9 dynamic-slice_bitcast_fusion.2
  188.2 3.8 collective-permute-done
  193.4 5.9 collective-permute-start
  200.0 0.7 constant_dynamic-slice_fusion.4
  201.4 0.9 dynamic-slice_bitcast_fusion.2
  202.3 3.8 collective-permute-done
  207.5 5.9 collective-permute-start
  214.0 0.7 constant_dynamic-slice_fusion.4
  215.5 0.9 dynamic-slice_bitcast_fusion.2
  216.3 3.8 collective-permute-done
  221.6 5.9 collective-permute-start
  228.1 0.7 constant_dynamic-slice_fusion.4
  229.6 0.9 dynamic-slice_bitcast_fusion.2
  230.4 3.8 collective-permute-done
  235.6 5.9 collective-permute-start
  242.2 0.7 constant_dynamic-slice_fusion.4
  243.6 0.9 dynamic-slice_bitcast_fusion.2
  244.5 3.8 collective-permute-done
  249.7 1.3 copy.10
  251.2 97.1 %all-reduce.3.cloned.1.call-done = f32[1024,256]{1,0:T(8,128)} async-done(((f32[1024,256]{1,0:T(8,128)}), f32[1024,256]{1,0:T(8,128)}) %all-reduce.3.cloned.1.call-update) | async-done | bytes 1048592 | tf_op jit(solution)/shard_map/psum | solution.py:65
  348.3 1.9 convolution_bitcast_fusion
  350.2 1.8 convolution_convert_fusion
  352.0 460.6 %all-reduce.5.cloned.1.call-done = f32[256,256]{0,1:T(8,128)} async-done(((f32[256,256]{0,1:T(8,128)}), f32[256,256]{0,1:T(8,128)}) %all-reduce.5.cloned.1.call-update) | async-done | bytes 262160 | tf_op jit(solution)/shard_map/psum | solution.py:75
  812.6 1.0 broadcast_multiply_fusion
  813.6 0.8 copy.11
  (99 shorter events, 21.4 us)
Async XLA Ops:
  7.2 343.1 %copy-start = (bf16[256,256]{1,0:T(8,128)(2,1)S(1)}, bf16[256,256]{1,0:T(8,128)(2,1)}, u32[]{:S(2)}) copy-start(bf16[256,256]{1,0:T(8,128)(2,1)} %param.13) | copy-start | bytes 393220
  7.2 341.1 %all-reduce.3.cloned.1.call-start = ((), (), s32[]{:S(2)}) async-start(), calls=%async_computation | async-start | bytes 2097152 | tf_op jit(solution)/shard_map/psum | solution.py:65
  7.9 35.6 %copy-start.1 = (bf16[1024,256]{1,0:T(8,128)(2,1)S(1)}, bf16[1024,256]{1,0:T(8,128)(2,1)}, u32[]{:S(2)}) copy-start(bf16[1024,256]{1,0:T(8,128)(2,1)} %param.12) | copy-start | bytes 1572868
  9.3 34.2 %collective-permute-start.1 = (bf16[1024,256]{1,0:T(8,128)(2,1)S(1)}, bf16[1024,256]{1,0:T(8,128)(2,1)S(1)}, u32[]{:S(2)}, u32[]{:S(2)}) collective-permute-start(bf16[1024,256]{1,0:T(8,128)(2,1)S(1)} %multiply_convert_fusion), channel_id=1, source_target_pairs={{64,0},{72,8},{80,16},{88,24},{96,32},{104,40},{112,48},{120,56},{... | collective-permute-start | bytes 1572872 | tf_op jit(solution)/shard_map/ppermute | solution.py:11
  43.8 47.2 %collective-permute-start.2 = (bf16[1024,256]{1,0:T(8,128)(2,1)S(1)}, bf16[1024,256]{1,0:T(8,128)(2,1)S(1)}, u32[]{:S(2)}, u32[]{:S(2)}) collective-permute-start(bf16[1024,256]{1,0:T(8,128)(2,1)S(1)} %broadcast_select_fusion), channel_id=1, source_target_pairs={{128,0},{136,8},{144,16},{152,24},{160,32},{168,40},{176,48},{184,... | collective-permute-start | bytes 1572872 | tf_op jit(solution)/shard_map/ppermute | solution.py:11
  91.1 35.7 %collective-permute-start.3 = (bf16[1024,256]{1,0:T(8,128)(2,1)S(1)}, bf16[1024,256]{1,0:T(8,128)(2,1)S(1)}, u32[]{:S(2)}, u32[]{:S(2)}) collective-permute-start(bf16[1024,256]{1,0:T(8,128)(2,1)S(1)} %broadcast_select_fusion.1), channel_id=1, source_target_pairs={{256,0},{264,8},{272,16},{280,24},{288,32},{296,40},{304,48},{312,... | collective-permute-start | bytes 1572872 | tf_op jit(solution)/shard_map/ppermute | solution.py:11
  96.0 0.7 copy-start.3
  128.2 35.7 %collective-permute-start = (bf16[1024,256]{1,0:T(8,128)(2,1)S(1)}, bf16[1024,256]{1,0:T(8,128)(2,1)S(1)}, u32[]{:S(2)}, u32[]{:S(2)}) collective-permute-start(bf16[1024,256]{1,0:T(8,128)(2,1)S(1)} %get-tuple-element.308), channel_id=1, source_target_pairs={{8,0},{16,8},{24,16},{32,24},{40,32},{48,40},{56,48},{64,56},{72,6... | collective-permute-start | bytes 1572872 | tf_op jit(solution)/shard_map/while/body/eval_jaxpr/ppermute | solution.py:11
  165.3 12.6 %collective-permute-start = (bf16[1024,256]{1,0:T(8,128)(2,1)S(1)}, bf16[1024,256]{1,0:T(8,128)(2,1)S(1)}, u32[]{:S(2)}, u32[]{:S(2)}) collective-permute-start(bf16[1024,256]{1,0:T(8,128)(2,1)S(1)} %get-tuple-element.308), channel_id=1, source_target_pairs={{8,0},{16,8},{24,16},{32,24},{40,32},{48,40},{56,48},{64,56},{72,6... | collective-permute-start | bytes 1572872 | tf_op jit(solution)/shard_map/while/body/eval_jaxpr/ppermute | solution.py:11
  179.4 12.6 %collective-permute-start = (bf16[1024,256]{1,0:T(8,128)(2,1)S(1)}, bf16[1024,256]{1,0:T(8,128)(2,1)S(1)}, u32[]{:S(2)}, u32[]{:S(2)}) collective-permute-start(bf16[1024,256]{1,0:T(8,128)(2,1)S(1)} %get-tuple-element.308), channel_id=1, source_target_pairs={{8,0},{16,8},{24,16},{32,24},{40,32},{48,40},{56,48},{64,56},{72,6... | collective-permute-start | bytes 1572872 | tf_op jit(solution)/shard_map/while/body/eval_jaxpr/ppermute | solution.py:11
  193.4 12.6 %collective-permute-start = (bf16[1024,256]{1,0:T(8,128)(2,1)S(1)}, bf16[1024,256]{1,0:T(8,128)(2,1)S(1)}, u32[]{:S(2)}, u32[]{:S(2)}) collective-permute-start(bf16[1024,256]{1,0:T(8,128)(2,1)S(1)} %get-tuple-element.308), channel_id=1, source_target_pairs={{8,0},{16,8},{24,16},{32,24},{40,32},{48,40},{56,48},{64,56},{72,6... | collective-permute-start | bytes 1572872 | tf_op jit(solution)/shard_map/while/body/eval_jaxpr/ppermute | solution.py:11
  207.5 12.6 %collective-permute-start = (bf16[1024,256]{1,0:T(8,128)(2,1)S(1)}, bf16[1024,256]{1,0:T(8,128)(2,1)S(1)}, u32[]{:S(2)}, u32[]{:S(2)}) collective-permute-start(bf16[1024,256]{1,0:T(8,128)(2,1)S(1)} %get-tuple-element.308), channel_id=1, source_target_pairs={{8,0},{16,8},{24,16},{32,24},{40,32},{48,40},{56,48},{64,56},{72,6... | collective-permute-start | bytes 1572872 | tf_op jit(solution)/shard_map/while/body/eval_jaxpr/ppermute | solution.py:11
  221.6 12.6 %collective-permute-start = (bf16[1024,256]{1,0:T(8,128)(2,1)S(1)}, bf16[1024,256]{1,0:T(8,128)(2,1)S(1)}, u32[]{:S(2)}, u32[]{:S(2)}) collective-permute-start(bf16[1024,256]{1,0:T(8,128)(2,1)S(1)} %get-tuple-element.308), channel_id=1, source_target_pairs={{8,0},{16,8},{24,16},{32,24},{40,32},{48,40},{56,48},{64,56},{72,6... | collective-permute-start | bytes 1572872 | tf_op jit(solution)/shard_map/while/body/eval_jaxpr/ppermute | solution.py:11
  235.6 12.6 %collective-permute-start = (bf16[1024,256]{1,0:T(8,128)(2,1)S(1)}, bf16[1024,256]{1,0:T(8,128)(2,1)S(1)}, u32[]{:S(2)}, u32[]{:S(2)}) collective-permute-start(bf16[1024,256]{1,0:T(8,128)(2,1)S(1)} %get-tuple-element.308), channel_id=1, source_target_pairs={{8,0},{16,8},{24,16},{32,24},{40,32},{48,40},{56,48},{64,56},{72,6... | collective-permute-start | bytes 1572872 | tf_op jit(solution)/shard_map/while/body/eval_jaxpr/ppermute | solution.py:11
  251.0 97.3 %copy-start.2 = (bf16[128,256]{1,0:T(8,128)(2,1)S(1)}, bf16[128,256]{1,0:T(8,128)(2,1)}, u32[]{:S(2)}) copy-start(bf16[128,256]{1,0:T(8,128)(2,1)} %param.11) | copy-start | bytes 196612
  251.0 561.5 %all-reduce.5.cloned.1.call-start = ((), (), s32[]{:S(2)}) async-start(), calls=%async_computation.1 | async-start | bytes 524288 | tf_op jit(solution)/shard_map/psum | solution.py:75
Sparse Core Ops, SparseCore 0:
  251.2 97.1 all-reduce.2
  354.3 458.2 all-reduce.4
where the time goes:
time: 822 us; the launch traced here: 821 us
  waiting for transfers between devices  675 us (82%)
  starting transfers between devices  87.8 us (11%)
  local copies, waits for them, and re-layouts  24.9 us (3%)
  between operations  14.2 us (2%)
  matrix products  9.97 us (1%)
  other arithmetic  8.83 us (1%)
    psum x1, waiting for transfers between devices, per_device(): lax.psum(weight_term, ('blk', 'rep')) * (1.0 / math.sqrt(node_total))  461 us
    ppermute x10, waiting for transfers between devices, from_behind(): return lax.ppermute(block, axis, route)  117 us
    psum x1, waiting for transfers between devices, per_device(): whole_sums = lax.psum(partial_sums, 'rep')  97.1 us
    ppermute x10, starting transfers between devices, from_behind(): return lax.ppermute(block, axis, route)  87.7 us
  transfers between devices with their start and end apart: 12, of which 12 were waited for; matrix products, arithmetic and copies ran while one was open for 3% of the time, Pallas kernels for 0%

commit v1 on v0

--- a/solution.py
+++ b/solution.py
@@ -62,7 +62,7 @@
     partial_sums = accumulated.reshape(slab_rows, width)
     share_rows = slab_rows // group_size
     share_root = lax.dynamic_slice_in_dim(inverse_root, rep_index * share_rows, share_rows, 0)
-    whole_sums = lax.psum(partial_sums, "rep")
+    whole_sums = lax.all_gather(partial_sums, "rep").sum(axis=0)
     own_sums = lax.dynamic_slice_in_dim(whole_sums, rep_index * share_rows, share_rows, 0)
     aggregated = (own_sums * share_root[:, None]).astype(jnp.bfloat16)
     input_grad = lax.dot_general(

time: 822 us -> 838 us (1.019)
  waiting for transfers between devices: 675 us -> 717 us
  starting transfers between devices: 87.8 us -> 58 us
    all_gather x0 -> x1, waiting for transfers between devices: none -> 114 us  [per_device(): whole_sums = lax.all_gather(partial_sums, 'rep').sum(axis=0)]
    psum x1 -> x0, waiting for transfers between devices: 97.1 us -> none  [per_device(): whole_sums = lax.psum(partial_sums, 'rep')]
    ppermute x10, starting transfers between devices: 87.7 us -> 58 us  [from_behind(): return lax.ppermute(block, axis, route)]
    ppermute x10, waiting for transfers between devices: 117 us -> 146 us  [from_behind(): return lax.ppermute(block, axis, route)]
where the time goes in v1:
time: 838 us; the launch traced here: 836 us
  waiting for transfers between devices  717 us (86%)
  starting transfers between devices  58 us (7%)
  local copies, waits for them, and re-layouts  24.3 us (3%)
  other arithmetic  14.4 us (2%)
  between operations  14.2 us (2%)
    psum x1, waiting for transfers between devices, per_device(): lax.psum(weight_term, ('blk', 'rep')) * (1.0 / math.sqrt(node_total))  457 us
    ppermute x10, waiting for transfers between devices, from_behind(): return lax.ppermute(block, axis, route)  146 us
    all_gather x1, waiting for transfers between devices, per_device(): whole_sums = lax.all_gather(partial_sums, 'rep').sum(axis=0)  114 us
    ppermute x10, starting transfers between devices, from_behind(): return lax.ppermute(block, axis, route)  58 us
  transfers between devices with their start and end apart: 12, of which 12 were waited for; matrix products, arithmetic and copies ran while one was open for 3% of the time, Pallas kernels for 0%

profile of v1, /device:TPU:4, one launch (start us, length us, event | category | flops | bytes accessed | tf_op | source)
XLA Modules:
  0.0 836.5 jit_solution(6066579211144297636)
XLA Ops:
  7.2 0.7 convert_rsqrt_fusion
  7.9 1.2 multiply_convert_fusion
  9.2 11.8 %collective-permute-start.1 = (bf16[1024,256]{1,0:T(8,128)(2,1)S(1)}, bf16[1024,256]{1,0:T(8,128)(2,1)S(1)}, u32[]{:S(2)}, u32[]{:S(2)}) collective-permute-start(bf16[1024,256]{1,0:T(8,128)(2,1)S(1)} %multiply_convert_fusion), channel_id=1, source_target_pairs={{64,0},{72,8},{80,16},{88,24},{96,32},{104,40},{112,48},{120,56},{... | collective-permute-start | bytes 1572872 | tf_op jit(solution)/shard_map/ppermute | solution.py:11
  21.0 22.4 %collective-permute-done.1 = bf16[1024,256]{1,0:T(8,128)(2,1)S(1)} collective-permute-done((bf16[1024,256]{1,0:T(8,128)(2,1)S(1)}, bf16[1024,256]{1,0:T(8,128)(2,1)S(1)}, u32[]{:S(2)}, u32[]{:S(2)}) %collective-permute-start.1) | collective-permute-done | bytes 524320 | tf_op jit(solution)/shard_map/ppermute | solution.py:11
  43.4 1.3 broadcast_select_fusion
  44.8 6.3 collective-permute-start.2
  51.2 0.7 compare_and_fusion.1
  51.9 62.4 %collective-permute-done.2 = bf16[1024,256]{1,0:T(8,128)(2,1)S(1)} collective-permute-done((bf16[1024,256]{1,0:T(8,128)(2,1)S(1)}, bf16[1024,256]{1,0:T(8,128)(2,1)S(1)}, u32[]{:S(2)}, u32[]{:S(2)}) %collective-permute-start.2) | collective-permute-done | bytes 524320 | tf_op jit(solution)/shard_map/ppermute | solution.py:11
  114.3 1.9 collective-permute-start.3
  116.9 0.7 slice_bitcast_fusion.2
  117.6 0.8 slice_bitcast_fusion.1
  118.4 34.3 %collective-permute-done.3 = bf16[1024,256]{1,0:T(8,128)(2,1)S(1)} collective-permute-done((bf16[1024,256]{1,0:T(8,128)(2,1)S(1)}, bf16[1024,256]{1,0:T(8,128)(2,1)S(1)}, u32[]{:S(2)}, u32[]{:S(2)}) %collective-permute-start.3) | collective-permute-done | bytes 524320 | tf_op jit(solution)/shard_map/ppermute | solution.py:11
  154.2 94.8 %while.20 = (s32[]{:T(128)}, bf16[1024,256]{1,0:T(8,128)(2,1)S(1)}, f32[8,128,256]{2,0,1:T(8,128)S(1)}, s32[1,8,2,8]{3,2,1,0:T(2,128)}, s32[1,8]{1,0:T(1,128)S(1...) while((s32[]{:T(128)}, bf16[1024,256]{1,0:T(8,128)(2,1)S(1)}, ...), condition=%wide.region_1.3_spmd.clone.clone, body=%wide.region_0.2_spmd.clone.clone.sunk | while | flops 72221880 | bytes 8067647 | solution.py:61
  154.2 2.3 collective-permute-start
  157.1 0.7 constant_dynamic-slice_fusion.4
  158.6 0.9 dynamic-slice_bitcast_fusion.2
  159.4 3.8 collective-permute-done
  164.7 5.9 collective-permute-start
  171.2 0.7 constant_dynamic-slice_fusion.4
  172.6 0.9 dynamic-slice_bitcast_fusion.2
  173.5 3.8 collective-permute-done
  178.7 5.9 collective-permute-start
  185.2 0.7 constant_dynamic-slice_fusion.4
  186.7 0.9 dynamic-slice_bitcast_fusion.2
  187.6 3.8 collective-permute-done
  192.8 5.9 collective-permute-start
  199.3 0.7 constant_dynamic-slice_fusion.4
  200.8 0.9 dynamic-slice_bitcast_fusion.2
  201.6 3.8 collective-permute-done
  206.8 5.9 collective-permute-start
  214.8 0.9 dynamic-slice_bitcast_fusion.2
  215.7 3.8 collective-permute-done
  220.9 5.9 collective-permute-start
  227.4 0.7 constant_dynamic-slice_fusion.4
  228.9 0.9 dynamic-slice_bitcast_fusion.2
  229.7 3.8 collective-permute-done
  235.0 5.9 collective-permute-start
  241.5 0.7 constant_dynamic-slice_fusion.4
  243.0 0.9 dynamic-slice_bitcast_fusion.2
  243.8 3.8 collective-permute-done
  249.0 1.4 copy.14
  250.6 113.8 %all-gather.2.cloned.1.call-done = f32[8,1024,256]{2,1,0:T(8,128)} async-done(((f32[1,1024,256]{2,1,0:T(8,128)}), f32[8,1024,256]{2,1,0:T(8,128)}) %all-gather.2.cloned.1.call-update) | async-done | bytes 8388624 | tf_op jit(solution)/shard_map/all_gather | solution.py:65
  364.4 4.1 reduce_sum.9
  368.5 1.0 convolution_bitcast_fusion
  369.5 0.8 convolution_convert_fusion
  370.3 457.5 %all-reduce.2.cloned.1.call-done = f32[256,256]{0,1:T(8,128)} async-done(((f32[256,256]{0,1:T(8,128)}), f32[256,256]{0,1:T(8,128)}) %all-reduce.2.cloned.1.call-update) | async-done | bytes 262160 | tf_op jit(solution)/shard_map/psum | solution.py:75
  827.8 1.0 broadcast_multiply_fusion
  828.8 0.8 copy.15
  (98 shorter events, 22.4 us)
Async XLA Ops:
  7.2 362.3 %copy-start = (bf16[256,256]{1,0:T(8,128)(2,1)S(1)}, bf16[256,256]{1,0:T(8,128)(2,1)}, u32[]{:S(2)}) copy-start(bf16[256,256]{1,0:T(8,128)(2,1)} %param.13) | copy-start | bytes 393220
  7.2 147.0 %copy-start.2 = (s32[1,8]{1,0:T(1,128)S(1)}, s32[1,8]{1,0:T(1,128)}, u32[]{:S(2)}) copy-start(s32[1,8]{1,0:T(1,128)} %param.16) | copy-start | bytes 100
  7.2 357.2 %all-gather.2.cloned.1.call-start = ((), (), s32[]{:S(2)}) async-start(), calls=%async_computation | async-start | bytes 9437184 | tf_op jit(solution)/shard_map/all_gather | solution.py:65
  9.2 34.2 %collective-permute-start.1 = (bf16[1024,256]{1,0:T(8,128)(2,1)S(1)}, bf16[1024,256]{1,0:T(8,128)(2,1)S(1)}, u32[]{:S(2)}, u32[]{:S(2)}) collective-permute-start(bf16[1024,256]{1,0:T(8,128)(2,1)S(1)} %multiply_convert_fusion), channel_id=1, source_target_pairs={{64,0},{72,8},{80,16},{88,24},{96,32},{104,40},{112,48},{120,56},{... | collective-permute-start | bytes 1572872 | tf_op jit(solution)/shard_map/ppermute | solution.py:11
  44.8 69.5 %collective-permute-start.2 = (bf16[1024,256]{1,0:T(8,128)(2,1)S(1)}, bf16[1024,256]{1,0:T(8,128)(2,1)S(1)}, u32[]{:S(2)}, u32[]{:S(2)}) collective-permute-start(bf16[1024,256]{1,0:T(8,128)(2,1)S(1)} %broadcast_select_fusion), channel_id=1, source_target_pairs={{128,0},{136,8},{144,16},{152,24},{160,32},{168,40},{176,48},{184,... | collective-permute-start | bytes 1572872 | tf_op jit(solution)/shard_map/ppermute | solution.py:11
  114.3 38.5 %collective-permute-start.3 = (bf16[1024,256]{1,0:T(8,128)(2,1)S(1)}, bf16[1024,256]{1,0:T(8,128)(2,1)S(1)}, u32[]{:S(2)}, u32[]{:S(2)}) collective-permute-start(bf16[1024,256]{1,0:T(8,128)(2,1)S(1)} %broadcast_select_fusion.1), channel_id=1, source_target_pairs={{256,0},{264,8},{272,16},{280,24},{288,32},{296,40},{304,48},{312,... | collective-permute-start | bytes 1572872 | tf_op jit(solution)/shard_map/ppermute | solution.py:11
  154.2 9.0 %collective-permute-start = (bf16[1024,256]{1,0:T(8,128)(2,1)S(1)}, bf16[1024,256]{1,0:T(8,128)(2,1)S(1)}, u32[]{:S(2)}, u32[]{:S(2)}) collective-permute-start(bf16[1024,256]{1,0:T(8,128)(2,1)S(1)} %get-tuple-element.310), channel_id=1, source_target_pairs={{8,0},{16,8},{24,16},{32,24},{40,32},{48,40},{56,48},{64,56},{72,6... | collective-permute-start | bytes 1572872 | tf_op jit(solution)/shard_map/while/body/eval_jaxpr/ppermute | solution.py:11
  164.7 12.6 %collective-permute-start = (bf16[1024,256]{1,0:T(8,128)(2,1)S(1)}, bf16[1024,256]{1,0:T(8,128)(2,1)S(1)}, u32[]{:S(2)}, u32[]{:S(2)}) collective-permute-start(bf16[1024,256]{1,0:T(8,128)(2,1)S(1)} %get-tuple-element.310), channel_id=1, source_target_pairs={{8,0},{16,8},{24,16},{32,24},{40,32},{48,40},{56,48},{64,56},{72,6... | collective-permute-start | bytes 1572872 | tf_op jit(solution)/shard_map/while/body/eval_jaxpr/ppermute | solution.py:11
  178.7 12.6 %collective-permute-start = (bf16[1024,256]{1,0:T(8,128)(2,1)S(1)}, bf16[1024,256]{1,0:T(8,128)(2,1)S(1)}, u32[]{:S(2)}, u32[]{:S(2)}) collective-permute-start(bf16[1024,256]{1,0:T(8,128)(2,1)S(1)} %get-tuple-element.310), channel_id=1, source_target_pairs={{8,0},{16,8},{24,16},{32,24},{40,32},{48,40},{56,48},{64,56},{72,6... | collective-permute-start | bytes 1572872 | tf_op jit(solution)/shard_map/while/body/eval_jaxpr/ppermute | solution.py:11
  192.8 12.6 %collective-permute-start = (bf16[1024,256]{1,0:T(8,128)(2,1)S(1)}, bf16[1024,256]{1,0:T(8,128)(2,1)S(1)}, u32[]{:S(2)}, u32[]{:S(2)}) collective-permute-start(bf16[1024,256]{1,0:T(8,128)(2,1)S(1)} %get-tuple-element.310), channel_id=1, source_target_pairs={{8,0},{16,8},{24,16},{32,24},{40,32},{48,40},{56,48},{64,56},{72,6... | collective-permute-start | bytes 1572872 | tf_op jit(solution)/shard_map/while/body/eval_jaxpr/ppermute | solution.py:11
  206.8 12.6 %collective-permute-start = (bf16[1024,256]{1,0:T(8,128)(2,1)S(1)}, bf16[1024,256]{1,0:T(8,128)(2,1)S(1)}, u32[]{:S(2)}, u32[]{:S(2)}) collective-permute-start(bf16[1024,256]{1,0:T(8,128)(2,1)S(1)} %get-tuple-element.310), channel_id=1, source_target_pairs={{8,0},{16,8},{24,16},{32,24},{40,32},{48,40},{56,48},{64,56},{72,6... | collective-permute-start | bytes 1572872 | tf_op jit(solution)/shard_map/while/body/eval_jaxpr/ppermute | solution.py:11
  220.9 12.6 %collective-permute-start = (bf16[1024,256]{1,0:T(8,128)(2,1)S(1)}, bf16[1024,256]{1,0:T(8,128)(2,1)S(1)}, u32[]{:S(2)}, u32[]{:S(2)}) collective-permute-start(bf16[1024,256]{1,0:T(8,128)(2,1)S(1)} %get-tuple-element.310), channel_id=1, source_target_pairs={{8,0},{16,8},{24,16},{32,24},{40,32},{48,40},{56,48},{64,56},{72,6... | collective-permute-start | bytes 1572872 | tf_op jit(solution)/shard_map/while/body/eval_jaxpr/ppermute | solution.py:11
  235.0 12.6 %collective-permute-start = (bf16[1024,256]{1,0:T(8,128)(2,1)S(1)}, bf16[1024,256]{1,0:T(8,128)(2,1)S(1)}, u32[]{:S(2)}, u32[]{:S(2)}) collective-permute-start(bf16[1024,256]{1,0:T(8,128)(2,1)S(1)} %get-tuple-element.310), channel_id=1, source_target_pairs={{8,0},{16,8},{24,16},{32,24},{40,32},{48,40},{56,48},{64,56},{72,6... | collective-permute-start | bytes 1572872 | tf_op jit(solution)/shard_map/while/body/eval_jaxpr/ppermute | solution.py:11
  249.0 119.4 %copy-start.1 = (bf16[128,256]{1,0:T(8,128)(2,1)S(1)}, bf16[128,256]{1,0:T(8,128)(2,1)}, u32[]{:S(2)}) copy-start(bf16[128,256]{1,0:T(8,128)(2,1)} %param.11) | copy-start | bytes 196612
  250.5 577.4 %all-reduce.2.cloned.1.call-start = ((), (), s32[]{:S(2)}) async-start(), calls=%async_computation.1 | async-start | bytes 524288 | tf_op jit(solution)/shard_map/psum | solution.py:75
Sparse Core Ops, SparseCore 0:
  250.6 113.7 all-gather.1
  370.4 457.3 all-reduce.1
